TPU v7x, 128 devices: a whole 4x4x4 slice. The times are simulated.
128 devices in a mesh: section: 2 (over core), blk: 16 (over y, x), mp: 4 (over z).
Axes of the slice: x: 4, y: 4, z: 4, core: 2. Of those that a mesh axis runs over, the one named last changes fastest.
Arguments:
- patches: bfloat16 [256, 5120], P('section'), may hold values from -6 to 6
- merge_gain: float32 [1280], replicated, may hold values from 0.25 to 1.75
- merge_first: bfloat16 [5120, 5120], P(None, ('blk', 'mp')), may hold values from -0.078125 to 0.078125
- merge_second: bfloat16 [5120, 4096], P(('blk', 'mp')), may hold values from -0.078125 to 0.078125
- text_embeds: bfloat16 [4, 1024, 4096], P(None, 'blk', 'mp'), may hold values from -7 to 14
- positions: int32 [256], replicated, may hold values from 0 to 4095, as said below
- segments: int32 [4096], replicated, may hold values from 0 to 2, never falling along the last dimension, each value on 1 to 2048 neighbouring positions
- norm_gain: float32 [2, 4096], P('section'), may hold values from 0.25 to 1.75
- query_weight: bfloat16 [2, 4096, 4096], P('section', 'blk', 'mp'), may hold values from -1 to 1
- keyval_weight: bfloat16 [2, 4096, 4, 2, 128], P('section', 'blk', 'mp'), may hold values from -1 to 1
- out_weight: bfloat16 [2, 4096, 4096], P('section', 'mp', 'blk'), may hold values from -0.09375 to 0.09375
Outputs:
- hidden: bfloat16 [2, 4, 1024, 4096], P('section', None, 'blk', 'mp')
Inputs may be any that keep to these rules, and one draw needn't show every extreme that they name: `positions`: distinct and increasing.
All inputs are finite; a program needn't handle non-finite values.
Results may differ from a plain program's by a relative error of at most 0.015.
Values may be sent and summed in bfloat16 or wider, within the bound.
No kernel may reach another device: no remote copies, remote signals or barrier semaphores. Data moves between devices by JAX's collectives and lax.ppermute only.
A program may use at most 128 MiB of HBM per device.

v0:
```python
import jax
import jax.numpy as jnp
from jax import lax
from jax.sharding import PartitionSpec as P

epsilon = 1e-06
rope_base = 1000000.0


def shifted(value, axis, by):
    size = lax.axis_size(axis)
    pairs = [(i, i + by) for i in range(size) if 0 <= i + by < size]
    return lax.ppermute(value, axis, pairs)


def rope_tables(where_at, head_size):
    steps_half = jnp.arange(head_size // 2).astype(jnp.float32)
    inverse = jnp.exp(-jnp.log(rope_base) * 2.0 * steps_half / head_size)
    angles = where_at.astype(jnp.float32)[:, None] * inverse[None, :]
    return (jnp.cos(angles), jnp.sin(angles))


def rotate(values, cosine, sine):
    half = values.shape[-1] // 2
    first = values[..., :half]
    second = values[..., half:]
    cosine = cosine[:, None, :]
    sine = sine[:, None, :]
    return jnp.concatenate(
        [first * cosine - second * sine, second * cosine + first * sine], axis=-1
    )


def local(
    patches,
    merge_gain,
    merge_first,
    merge_second,
    text_embeds,
    positions,
    segments,
    norm_gain,
    query_weight,
    keyval_weight,
    out_weight,
):
    count = patches.shape[0]
    width = merge_gain.shape[0]
    blocks = text_embeds.shape[0]
    rows_here = text_embeds.shape[1]
    slice_width = text_embeds.shape[2]
    seq_len = segments.shape[0]
    block_len = seq_len // blocks
    section_index = lax.axis_index("section")
    cycle_index = lax.axis_index("blk")
    model_index = lax.axis_index("mp")
    pieces = patches.astype(jnp.float32).reshape(count, -1, width)
    centered = pieces - jnp.mean(pieces, axis=-1, keepdims=True)
    variance = jnp.mean(centered * centered, axis=-1, keepdims=True)
    normed = (
        (centered * lax.rsqrt(variance + epsilon) * merge_gain)
        .reshape(count, -1)
        .astype(jnp.bfloat16)
    )
    inner = jax.nn.gelu(
        jnp.dot(normed, merge_first, preferred_element_type=jnp.float32), approximate=False
    ).astype(jnp.bfloat16)
    partial_merge = jnp.dot(inner, merge_second, preferred_element_type=jnp.float32)
    merged_full = lax.psum(partial_merge, ("blk", "mp")).astype(jnp.bfloat16)
    merged_mine = lax.dynamic_slice_in_dim(merged_full, model_index * slice_width, slice_width, 1)
    visual_all = lax.all_gather(merged_mine, "section", axis=0, tiled=True)
    query_full, keyval_full, out_full = (
        lax.all_gather(query_weight, "blk", axis=1, tiled=True),
        lax.all_gather(keyval_weight, "blk", axis=1, tiled=True),
        lax.all_gather(out_weight, "blk", axis=2, tiled=True),
    )
    query_full = query_full[0]
    kv_heads = keyval_full.shape[2]
    head_size = keyval_full.shape[4]
    keyval_full = keyval_full[0].reshape(keyval_full.shape[1], -1)
    out_full = out_full[0]
    gain_here = norm_gain[0]
    group = query_full.shape[1] // (kv_heads * head_size)
    scale = 1.0 / head_size**0.5
    key_where = jnp.arange(seq_len)
    ticks = blocks + lax.axis_size("section") - 1
    zero_index = jnp.zeros((), jnp.int32)
    held = jnp.zeros((rows_here, slice_width), jnp.bfloat16)
    cache_keys = jnp.zeros((seq_len, kv_heads, head_size), jnp.bfloat16)
    cache_values = jnp.zeros((seq_len, kv_heads, head_size), jnp.bfloat16)
    outputs = jnp.zeros((blocks, rows_here, slice_width), jnp.bfloat16)
    for tick_now in range(ticks):
        bound = min(tick_now + 1, blocks) * block_len
        block_now = tick_now - section_index
        active = (block_now >= 0) & (block_now < blocks)
        block_safe = jnp.clip(block_now, 0, blocks - 1)
        row_where = block_safe * block_len + cycle_index * rows_here + jnp.arange(rows_here)
        is_visual = positions[None, :] == row_where[:, None]
        picked = jnp.dot(
            is_visual.astype(jnp.bfloat16), visual_all, preferred_element_type=jnp.float32
        ).astype(jnp.bfloat16)
        text_rows = lax.dynamic_index_in_dim(text_embeds, block_safe, 0, keepdims=False)
        embedded = jnp.where(jnp.any(is_visual, axis=1)[:, None], picked, text_rows)
        incoming = jnp.where(section_index == 0, embedded, held)
        features = lax.all_gather(incoming, "mp", axis=1, tiled=True)
        feat_f = features.astype(jnp.float32)
        normx = (
            feat_f
            * lax.rsqrt(jnp.mean(feat_f * feat_f, axis=-1, keepdims=True) + epsilon)
            * gain_here
        ).astype(jnp.bfloat16)
        cosine, sine = rope_tables(row_where, head_size)
        query = jnp.dot(normx, query_full, preferred_element_type=jnp.float32).reshape(
            rows_here, -1, head_size
        )
        query = (
            rotate(query, cosine, sine)
            .astype(jnp.bfloat16)
            .reshape(rows_here, kv_heads, group, head_size)
        )
        keyval = jnp.dot(normx, keyval_full, preferred_element_type=jnp.float32).reshape(
            rows_here, kv_heads, 2, head_size
        )
        new_keys = rotate(keyval[:, :, 0, :], cosine, sine).astype(jnp.bfloat16)
        new_values = keyval[:, :, 1, :].astype(jnp.bfloat16)
        block_keys, block_values = (
            lax.all_gather(new_keys, "blk", axis=0, tiled=True),
            lax.all_gather(new_values, "blk", axis=0, tiled=True),
        )
        start = block_safe * block_len
        cache_keys = jnp.where(
            active,
            lax.dynamic_update_slice(cache_keys, block_keys, (start, zero_index, zero_index)),
            cache_keys,
        )
        cache_values = jnp.where(
            active,
            lax.dynamic_update_slice(cache_values, block_values, (start, zero_index, zero_index)),
            cache_values,
        )
        keys_seen = cache_keys[:bound]
        values_seen = cache_values[:bound]
        scores = (
            jnp.einsum("qkgd,skd->kgqs", query, keys_seen, preferred_element_type=jnp.float32)
            * scale
        )
        row_segments = jnp.take(segments, row_where)
        allowed = (key_where[None, :bound] <= row_where[:, None]) & (
            segments[None, :bound] == row_segments[:, None]
        )
        scores = jnp.where(allowed[None, None], scores, -jnp.inf)
        top = jnp.max(scores, axis=-1, keepdims=True)
        expo = jnp.exp(scores - top)
        probs = (expo / jnp.sum(expo, axis=-1, keepdims=True)).astype(jnp.bfloat16)
        attended = jnp.einsum(
            "kgqs,skd->qkgd", probs, values_seen, preferred_element_type=jnp.float32
        )
        attended = attended.reshape(rows_here, -1).astype(jnp.bfloat16)
        term = jnp.dot(attended, out_full, preferred_element_type=jnp.float32)
        summed = lax.psum_scatter(
            term.astype(jnp.bfloat16), "mp", scatter_dimension=1, tiled=True
        ).astype(jnp.float32)
        result = (incoming.astype(jnp.float32) + summed).astype(jnp.bfloat16)
        outputs = jnp.where(
            active,
            lax.dynamic_update_slice(outputs, result[None], (block_safe, zero_index, zero_index)),
            outputs,
        )
        held = shifted(result, "section", 1)
    return outputs[None]


def solution(mesh):
    return jax.shard_map(
        local,
        mesh=mesh,
        in_specs=(
            P("section", None),
            P(),
            P(None, ("blk", "mp")),
            P(("blk", "mp"), None),
            P(None, "blk", "mp"),
            P(),
            P(),
            P("section", None),
            P("section", "blk", "mp"),
            P("section", "blk", "mp", None, None),
            P("section", "mp", "blk"),
        ),
        out_specs=P("section", None, "blk", "mp"),
        check_vma=False,
    )
```

profile of v0, /device:TPU:0, one launch (start us, length us, event | category | flops | bytes accessed | tf_op | source)
XLA Modules:
  0.0 948.9 jit_solution(6913599249277682439)
XLA Ops:
  8.8 2.9 reshape.1266
  16.2 5.2 fusion.210
  23.5 383.3 %all-reduce.1 = bf16[128,4096]{1,0:T(8,128)(2,1)S(1)} all-reduce(f32[128,4096]{1,0:T(8,128)} %fusion.210), channel_id=1, replica_groups=mesh['section'=2,'blk'=16,'mp'=4] {'blk','mp'}, use_global_device_ids=true, to_apply=%region_3.4 | all-reduce | flops 524288 | bytes 3145728 | tf_op jit(solution)/shard_map/psum | solution.py:69
  411.0 13.4 %all_gather.58 = bf16[64,4096]{1,0:T(8,128)(2,1)S(1)} all-gather(bf16[64,1024]{1,0:T(8,128)(2,1)S(1)} %fusion.63), channel_id=1, replica_groups=mesh['section'=2,'blk'=16,'mp'=4] {'mp'}, dimensions={1}, use_global_device_ids=true | all-gather | bytes 655360 | tf_op jit(solution)/shard_map/all_gather | solution.py:105
  426.1 4.7 copy.37
  432.0 20.7 %all_gather.61 = bf16[1024,1,128]{2,0,1:T(8,128)(2,1)S(1)} all-gather(bf16[64,1,128]{2,0,1:T(8,128)(2,1)S(1)} %pad_maximum_fusion), channel_id=1, replica_groups=mesh['section'=2,'blk'=16,'mp'=4] {'blk'}, dimensions={0}, use_global_device_ids=true | all-gather | bytes 278528 | tf_op jit(solution)/shard_map/all_gather | solution.py:127
  452.7 24.1 %all-gather = bf16[1024,1,1,128]{3,0,2,1:T(8,128)(2,1)S(1)} all-gather(bf16[64,1,1,128]{3,0,2,1:T(8,128)(2,1)S(1)} %slice.285), channel_id=2, replica_groups=mesh['section'=2,'blk'=16,'mp'=4] {'blk'}, dimensions={0}, use_global_device_ids=true | all-gather | bytes 278528 | tf_op jit(solution)/shard_map/all_gather | solution.py:128
  480.5 11.8 %copy.31 = bf16[1024,4096]{1,0:T(8,128)(2,1)} copy(bf16[1024,4096]{0,1:T(8,128)(2,1)} %bitcast.333) | data formatting | bytes 16777216 | tf_op jit(solution)/shard_map/dot_general | solution.py:113
  492.3 6.1 fusion.125
  502.2 5.8 fusion.13
  511.2 15.4 %reduce-scatter.6.cloned.1.call-done = bf16[64,1024]{1,0:T(8,128)(2,1)} async-done(((bf16[64,4096]{1,0:T(8,128)(2,1)}), bf16[64,1024]{1,0:T(8,128)(2,1)}) %reduce-scatter.6.cloned.1.call-update) | async-done | bytes 131088 | tf_op jit(solution)/shard_map/reduce_scatter | solution.py:160
  531.9 13.5 %all_gather.64 = bf16[64,4096]{1,0:T(8,128)(2,1)S(1)} all-gather(bf16[64,1024]{1,0:T(8,128)(2,1)S(1)} %fusion.65), channel_id=1, replica_groups=mesh['section'=2,'blk'=16,'mp'=4] {'mp'}, dimensions={1}, use_global_device_ids=true | all-gather | bytes 655360 | tf_op jit(solution)/shard_map/all_gather | solution.py:105
  546.5 6.1 fusion.128
  552.6 23.8 %all-gather.1 = bf16[1024,1,1,128]{3,0,2,1:T(8,128)(2,1)S(1)} all-gather(bf16[64,1,1,128]{3,0,2,1:T(8,128)(2,1)S(1)} %slice.284), channel_id=3, replica_groups=mesh['section'=2,'blk'=16,'mp'=4] {'blk'}, dimensions={0}, use_global_device_ids=true | all-gather | bytes 278528 | tf_op jit(solution)/shard_map/all_gather | solution.py:128
  576.7 23.3 %all_gather.66 = bf16[1024,1,128]{2,0,1:T(8,128)(2,1)S(1)} all-gather(bf16[64,1,128]{2,0,1:T(8,128)(2,1)S(1)} %pad_maximum_fusion.1), channel_id=1, replica_groups=mesh['section'=2,'blk'=16,'mp'=4] {'blk'}, dimensions={0}, use_global_device_ids=true | all-gather | bytes 278528 | tf_op jit(solution)/shard_map/all_gather | solution.py:127
  616.2 14.5 %reduce-scatter.8.cloned.1.call-done = bf16[64,1024]{1,0:T(8,128)(2,1)} async-done(((bf16[64,4096]{1,0:T(8,128)(2,1)}), bf16[64,1024]{1,0:T(8,128)(2,1)}) %reduce-scatter.8.cloned.1.call-update) | async-done | bytes 131088 | tf_op jit(solution)/shard_map/reduce_scatter | solution.py:160
  633.9 13.5 %all_gather.67 = bf16[64,4096]{1,0:T(8,128)(2,1)S(1)} all-gather(bf16[64,1024]{1,0:T(8,128)(2,1)S(1)} %broadcast_select_fusion.2), channel_id=1, replica_groups=mesh['section'=2,'blk'=16,'mp'=4] {'mp'}, dimensions={1}, use_global_device_ids=true | all-gather | bytes 655360 | tf_op jit(solution)/shard_map/all_gather | solution.py:105
  648.5 6.1 fusion.131
  654.6 23.8 %all-gather.2 = bf16[1024,1,1,128]{3,0,2,1:T(8,128)(2,1)S(1)} all-gather(bf16[64,1,1,128]{3,0,2,1:T(8,128)(2,1)S(1)} %slice.283), channel_id=4, replica_groups=mesh['section'=2,'blk'=16,'mp'=4] {'blk'}, dimensions={0}, use_global_device_ids=true | all-gather | bytes 278528 | tf_op jit(solution)/shard_map/all_gather | solution.py:128
  678.7 23.4 %all_gather.69 = bf16[1024,1,128]{2,0,1:T(8,128)(2,1)S(1)} all-gather(bf16[64,1,128]{2,0,1:T(8,128)(2,1)S(1)} %pad_maximum_fusion.2), channel_id=1, replica_groups=mesh['section'=2,'blk'=16,'mp'=4] {'blk'}, dimensions={0}, use_global_device_ids=true | all-gather | bytes 278528 | tf_op jit(solution)/shard_map/all_gather | solution.py:127
  715.8 17.7 %reduce-scatter.10.cloned.1.call-done = bf16[64,1024]{1,0:T(8,128)(2,1)} async-done(((bf16[64,4096]{1,0:T(8,128)(2,1)}), bf16[64,1024]{1,0:T(8,128)(2,1)}) %reduce-scatter.10.cloned.1.call-update) | async-done | bytes 131088 | tf_op jit(solution)/shard_map/reduce_scatter | solution.py:160
  737.7 13.4 %all_gather.70 = bf16[64,4096]{1,0:T(8,128)(2,1)S(1)} all-gather(bf16[64,1024]{1,0:T(8,128)(2,1)S(1)} %broadcast_select_fusion.1), channel_id=1, replica_groups=mesh['section'=2,'blk'=16,'mp'=4] {'mp'}, dimensions={1}, use_global_device_ids=true | all-gather | bytes 655360 | tf_op jit(solution)/shard_map/all_gather | solution.py:105
  752.1 6.1 fusion.134
  758.2 23.8 %all-gather.3 = bf16[1024,1,1,128]{3,0,2,1:T(8,128)(2,1)S(1)} all-gather(bf16[64,1,1,128]{3,0,2,1:T(8,128)(2,1)S(1)} %slice.282), channel_id=5, replica_groups=mesh['section'=2,'blk'=16,'mp'=4] {'blk'}, dimensions={0}, use_global_device_ids=true | all-gather | bytes 278528 | tf_op jit(solution)/shard_map/all_gather | solution.py:128
  782.3 23.2 %all_gather.72 = bf16[1024,1,128]{2,0,1:T(8,128)(2,1)S(1)} all-gather(bf16[64,1,128]{2,0,1:T(8,128)(2,1)S(1)} %pad_maximum_fusion.3), channel_id=1, replica_groups=mesh['section'=2,'blk'=16,'mp'=4] {'blk'}, dimensions={0}, use_global_device_ids=true | all-gather | bytes 278528 | tf_op jit(solution)/shard_map/all_gather | solution.py:127
  809.1 2.9 fusion.314
  818.7 18.8 %reduce-scatter.12.cloned.1.call-done = bf16[64,1024]{1,0:T(8,128)(2,1)} async-done(((bf16[64,4096]{1,0:T(8,128)(2,1)}), bf16[64,1024]{1,0:T(8,128)(2,1)}) %reduce-scatter.12.cloned.1.call-update) | async-done | bytes 131088 | tf_op jit(solution)/shard_map/reduce_scatter | solution.py:160
  844.1 12.8 %all_gather.73 = bf16[64,4096]{1,0:T(8,128)(2,1)S(1)} all-gather(bf16[64,1024]{1,0:T(8,128)(2,1)S(1)} %broadcast_select_fusion), channel_id=1, replica_groups=mesh['section'=2,'blk'=16,'mp'=4] {'mp'}, dimensions={1}, use_global_device_ids=true | all-gather | bytes 655360 | tf_op jit(solution)/shard_map/all_gather | solution.py:105
  857.9 6.1 fusion.137
  864.0 23.8 %all-gather.4 = bf16[1024,1,1,128]{3,0,2,1:T(8,128)(2,1)S(1)} all-gather(bf16[64,1,1,128]{3,0,2,1:T(8,128)(2,1)S(1)} %slice.281), channel_id=6, replica_groups=mesh['section'=2,'blk'=16,'mp'=4] {'blk'}, dimensions={0}, use_global_device_ids=true | all-gather | bytes 278528 | tf_op jit(solution)/shard_map/all_gather | solution.py:128
  888.0 23.3 %all_gather.75 = bf16[1024,1,128]{2,0,1:T(8,128)(2,1)S(1)} all-gather(bf16[64,1,128]{2,0,1:T(8,128)(2,1)S(1)} %pad_maximum_fusion.4), channel_id=1, replica_groups=mesh['section'=2,'blk'=16,'mp'=4] {'blk'}, dimensions={0}, use_global_device_ids=true | all-gather | bytes 278528 | tf_op jit(solution)/shard_map/all_gather | solution.py:127
  922.1 18.1 %reduce-scatter.14.cloned.1.call-done = bf16[64,1024]{1,0:T(8,128)(2,1)} async-done(((bf16[64,4096]{1,0:T(8,128)(2,1)}), bf16[64,1024]{1,0:T(8,128)(2,1)}) %reduce-scatter.14.cloned.1.call-update) | async-done | bytes 131088 | tf_op jit(solution)/shard_map/reduce_scatter | solution.py:160
  (308 shorter events, 102.9 us)
Async XLA Ops:
  6.5 419.6 %all-gather.9.cloned.1.call-start = ((), (), s32[]{:S(2)}) async-start(), calls=%async_computation.5 | async-start | bytes 2228224 | tf_op jit(solution)/shard_map/all_gather | solution.py:74
  7.3 473.2 %all-gather.11.cloned.1.call-start = ((), (), s32[]{:S(2)}) async-start(), calls=%async_computation.6 | async-start | bytes 8912896 | tf_op jit(solution)/shard_map/all_gather | solution.py:73
  8.0 494.1 %all-gather.13.cloned.1.call-start = ((), (), s32[]{:S(2)}) async-start(), calls=%async_computation.7 | async-start | bytes 8912896 | tf_op jit(solution)/shard_map/all_gather | solution.py:75
  8.7 517.9 %reduce-scatter.6.cloned.1.call-start = ((), (), s32[]{:S(2)}) async-start(), calls=%async_computation.8 | async-start | bytes 655360 | tf_op jit(solution)/shard_map/reduce_scatter | solution.py:160
  21.4 385.4 %copy-start.25 = (s32[256]{0:T(256)S(1)}, s32[256]{0:T(256)}, u32[]{:S(2)}) copy-start(s32[256]{0:T(256)} %param.18) | copy-start | bytes 3076
  21.4 403.2 %slice-start.8 = ((s32[4096]{0:T(1024)}), s32[1024]{0:T(1024)S(1)}, s32[]{:S(2)}) async-start(s32[4096]{0:T(1024)} %param.19), calls=%async_computation.21 | async-start | bytes 8192 | tf_op jit(solution)/shard_map/slice | solution.py:149
  21.4 404.6 %copy-start.46 = (f32[64]{0:T(128)}, f32[64]{0:T(128)S(1)}, u32[]{:S(2)}) copy-start(f32[64]{0:T(128)S(1)} %get-tuple-element.74) | copy-start | bytes 772
  22.2 554.2 %copy-start.26 = (f32[64]{0:T(128)}, f32[64]{0:T(128)S(1)}, u32[]{:S(2)}) copy-start(f32[64]{0:T(128)S(1)} %multiply_exponential_fusion) | copy-start | bytes 772
  22.2 384.6 %copy-start.44 = (s32[64]{0:T(128)}, s32[64]{0:T(128)S(1)}, u32[]{:S(2)}) copy-start(s32[64]{0:T(128)S(1)} %iota_add_fusion.5) | copy-start | bytes 772
  22.3 384.5 %copy-start.29 = (s32[64]{0:T(128)}, s32[64]{0:T(128)S(1)}, u32[]{:S(2)}) copy-start(s32[64]{0:T(128)S(1)} %get-tuple-element.77) | copy-start | bytes 772
  22.3 403.8 %copy-start.40 = (f32[64]{0:T(128)}, f32[64]{0:T(128)S(1)}, u32[]{:S(2)}) copy-start(f32[64]{0:T(128)S(1)} %get-tuple-element.80) | copy-start | bytes 772
  22.3 403.8 %copy-start.42 = (f32[64]{0:T(128)}, f32[64]{0:T(128)S(1)}, u32[]{:S(2)}) copy-start(f32[64]{0:T(128)S(1)} %get-tuple-element.79) | copy-start | bytes 772
  22.3 384.5 %copy-start.32 = (s32[64]{0:T(128)}, s32[64]{0:T(128)S(1)}, u32[]{:S(2)}) copy-start(s32[64]{0:T(128)S(1)} %get-tuple-element.75) | copy-start | bytes 772
  22.3 384.5 %copy-start.34 = (s32[64]{0:T(128)}, s32[64]{0:T(128)S(1)}, u32[]{:S(2)}) copy-start(s32[64]{0:T(128)S(1)} %get-tuple-element.76) | copy-start | bytes 772
  22.3 403.7 %copy-start.36 = (f32[64]{0:T(128)}, f32[64]{0:T(128)S(1)}, u32[]{:S(2)}) copy-start(f32[64]{0:T(128)S(1)} %get-tuple-element.82) | copy-start | bytes 772
  22.4 403.7 %copy-start.38 = (f32[64]{0:T(128)}, f32[64]{0:T(128)S(1)}, u32[]{:S(2)}) copy-start(f32[64]{0:T(128)S(1)} %get-tuple-element.81) | copy-start | bytes 772
  508.0 122.6 %reduce-scatter.8.cloned.1.call-start = ((), (), s32[]{:S(2)}) async-start(), calls=%async_computation.9 | async-start | bytes 655360 | tf_op jit(solution)/shard_map/reduce_scatter | solution.py:160
  527.7 2.4 collective-permute-start
  546.5 56.9 %copy-start.21 = (f32[64,64]{1,0:T(8,128)S(1)}, f32[64,64]{1,0:T(8,128)}, u32[]{:S(2)}) copy-start(f32[64,64]{1,0:T(8,128)} %get-tuple-element.51) | copy-start | bytes 49156
  546.5 56.9 %copy-start.22 = (f32[64,64]{1,0:T(8,128)S(1)}, f32[64,64]{1,0:T(8,128)}, u32[]{:S(2)}) copy-start(f32[64,64]{1,0:T(8,128)} %get-tuple-element.52) | copy-start | bytes 49156
  546.5 57.1 %copy-start.14 = (pred[64,2048]{1,0:T(8,128)(4,1)S(1)}, pred[64,2048]{1,0:T(8,128)(4,1)}, u32[]{:S(2)}) copy-start(pred[64,2048]{1,0:T(8,128)(4,1)} %compare_and_fusion.1) | copy-start | bytes 393220
  611.8 121.7 %reduce-scatter.10.cloned.1.call-start = ((), (), s32[]{:S(2)}) async-start(), calls=%async_computation.10 | async-start | bytes 655360 | tf_op jit(solution)/shard_map/reduce_scatter | solution.py:160
  631.6 2.3 collective-permute-start.1
  648.5 57.1 %copy-start.19 = (f32[64,64]{1,0:T(8,128)S(1)}, f32[64,64]{1,0:T(8,128)}, u32[]{:S(2)}) copy-start(f32[64,64]{1,0:T(8,128)} %get-tuple-element.53) | copy-start | bytes 49156
  648.5 57.1 %copy-start.20 = (f32[64,64]{1,0:T(8,128)S(1)}, f32[64,64]{1,0:T(8,128)}, u32[]{:S(2)}) copy-start(f32[64,64]{1,0:T(8,128)} %get-tuple-element.54) | copy-start | bytes 49156
  648.5 57.2 %copy-start.13 = (pred[64,3072]{1,0:T(8,128)(4,1)S(1)}, pred[64,3072]{1,0:T(8,128)(4,1)}, u32[]{:S(2)}) copy-start(pred[64,3072]{1,0:T(8,128)(4,1)} %compare_and_fusion) | copy-start | bytes 589828
  714.5 122.9 %reduce-scatter.12.cloned.1.call-start = ((), (), s32[]{:S(2)}) async-start(), calls=%async_computation.11 | async-start | bytes 655360 | tf_op jit(solution)/shard_map/reduce_scatter | solution.py:160
  734.5 2.5 collective-permute-start.2
  752.1 56.9 %copy-start.17 = (f32[64,64]{1,0:T(8,128)S(1)}, f32[64,64]{1,0:T(8,128)}, u32[]{:S(2)}) copy-start(f32[64,64]{1,0:T(8,128)} %get-tuple-element.55) | copy-start | bytes 49156
  752.1 57.0 %copy-start.3 = (pred[64,4096]{1,0:T(8,128)(4,1)S(1)}, pred[64,4096]{1,0:T(8,128)(4,1)}, u32[]{:S(2)}) copy-start(pred[64,4096]{1,0:T(8,128)(4,1)} %get-tuple-element.40) | copy-start | bytes 786436
  818.6 121.5 %reduce-scatter.14.cloned.1.call-start = ((), (), s32[]{:S(2)}) async-start(), calls=%async_computation.12 | async-start | bytes 655360 | tf_op jit(solution)/shard_map/reduce_scatter | solution.py:160
  838.5 4.9 collective-permute-start.3
  (50 other events, 668.7 us)
Sparse Core Ops, SparseCore 0:
  9.5 47.7 all-gather.8
  59.5 74.0 all-gather.10
  135.7 81.8 all-gather.12
  508.1 18.4 reduce-scatter.5
  611.9 18.7 reduce-scatter.7
  714.6 18.8 reduce-scatter.9
  818.8 18.6 reduce-scatter.11
  921.4 18.7 reduce-scatter.13
where the time goes:
time: 957 us; the launch traced here: 949 us
  blocking collectives  685 us (72%)
  waiting for transfers between devices  87 us (9%)
  matrix products  81.5 us (9%)
  other arithmetic  37.5 us (4%)
  local copies, waits for them, and re-layouts  37.3 us (4%)
  between operations  15.1 us (2%)
    psum x1, blocking collectives, local(): merged_full = lax.psum(partial_merge, ('blk', 'mp')).astype(jnp.bfloat16)  383 us
    all_gather x5, blocking collectives, local(): lax.all_gather(new_values, 'blk', axis=0, tiled=True)  119 us
    all_gather x5, blocking collectives, local(): lax.all_gather(new_keys, 'blk', axis=0, tiled=True)  114 us
    reduce_scatter x5, waiting for transfers between devices, local(): lax.psum_scatter(term.astype(jnp.bfloat16), 'mp', scatter_dimension=1, ti...  84.4 us
    all_gather x5, blocking collectives, local(): features = lax.all_gather(incoming, 'mp', axis=1, tiled=True)  66.5 us
    dot_general x5, matrix products, local(): jnp.dot(normx, query_full, preferred_element_type=jnp.float32)  30.4 us
  transfers between devices with their start and end apart: 12, of which 6 were waited for; matrix products, arithmetic and copies ran while one was open for 7% of the time, Pallas kernels for 0%

commit v1 on v0

--- a/solution.py
+++ b/solution.py
@@ -5,6 +5,11 @@
 
 epsilon = 1e-06
 rope_base = 1000000.0
+
+
+def one_after_other(x, leading, second_2):
+    partial = lax.psum(x, leading)
+    return lax.psum(partial, second_2)
 
 
 def shifted(value, axis, by):
@@ -66,7 +71,7 @@
         jnp.dot(normed, merge_first, preferred_element_type=jnp.float32), approximate=False
     ).astype(jnp.bfloat16)
     partial_merge = jnp.dot(inner, merge_second, preferred_element_type=jnp.float32)
-    merged_full = lax.psum(partial_merge, ("blk", "mp")).astype(jnp.bfloat16)
+    merged_full = one_after_other(partial_merge, "mp", "blk").astype(jnp.bfloat16)
     merged_mine = lax.dynamic_slice_in_dim(merged_full, model_index * slice_width, slice_width, 1)
     visual_all = lax.all_gather(merged_mine, "section", axis=0, tiled=True)
     query_full, keyval_full, out_full = (

time: 957 us -> 740 us (0.77)
  blocking collectives: 685 us -> 410 us
  waiting for transfers between devices: 87 us -> 142 us
    psum x1, blocking collectives: 383 us -> 109 us  [one_after_other(): return lax.psum(partial, second_2)]
    psum x0 -> x1, waiting for transfers between devices: none -> 55.4 us  [one_after_other(): partial = lax.psum(x, leading)]
  transfers between devices with their start and end apart: 12 -> 13, of which waited for: 6 -> 6; matrix products, arithmetic and copies ran while one was open for 7% -> 7% of each run, Pallas kernels for 0% -> 0%
where the time goes in v1:
time: 740 us; the launch traced here: 731 us
  blocking collectives  410 us (55%)
  waiting for transfers between devices  142 us (19%)
  matrix products  81.7 us (11%)
  other arithmetic  37.5 us (5%)
  local copies, waits for them, and re-layouts  37 us (5%)
  between operations  16.7 us (2%)
    all_gather x5, blocking collectives, local(): lax.all_gather(new_values, 'blk', axis=0, tiled=True)  119 us
    all_gather x5, blocking collectives, local(): lax.all_gather(new_keys, 'blk', axis=0, tiled=True)  114 us
    psum x1, blocking collectives, one_after_other(): return lax.psum(partial, second_2)  109 us
    reduce_scatter x5, waiting for transfers between devices, local(): lax.psum_scatter(term.astype(jnp.bfloat16), 'mp', scatter_dimension=1, ti...  85.1 us
    all_gather x5, blocking collectives, local(): features = lax.all_gather(incoming, 'mp', axis=1, tiled=True)  65.8 us
    psum x1, waiting for transfers between devices, one_after_other(): partial = lax.psum(x, leading)  55.4 us
    dot_general x5, matrix products, local(): jnp.dot(normx, query_full, preferred_element_type=jnp.float32)  30.4 us
    dot_general x5, matrix products, local(): term = jnp.dot(attended, out_full, preferred_element_type=jnp.float32)  15.2 us
  transfers between devices with their start and end apart: 13, of which 6 were waited for; matrix products, arithmetic and copies ran while one was open for 7% of the time, Pallas kernels for 0%

profile of v1, /device:TPU:0, one launch (start us, length us, event | category | flops | bytes accessed | tf_op | source)
XLA Modules:
  0.0 731.1 jit_solution(2510910053995191447)
XLA Ops:
  7.4 2.9 reshape.1266
  14.9 5.4 fusion.210
  26.5 55.4 %all-reduce.3.cloned.1.call-done = f32[128,4096]{1,0:T(8,128)} async-done(((f32[128,4096]{1,0:T(8,128)}), f32[128,4096]{1,0:T(8,128)}) %all-reduce.3.cloned.1.call-update) | async-done | bytes 2097168 | tf_op jit(solution)/shard_map/psum | solution.py:11
  81.9 108.8 %all-reduce.4 = bf16[128,4096]{1,0:T(8,128)(2,1)S(1)} all-reduce(f32[128,4096]{1,0:T(8,128)} %all-reduce.3.cloned.1.call-done), channel_id=1, replica_groups=mesh['section'=2,'blk'=16,'mp'=4] {'blk'}, use_global_device_ids=true, to_apply=%region_4.5 | all-reduce | flops 524288 | bytes 3145728 | tf_op jit(solution)/shard_map/psum | solution.py:12
  194.2 12.8 %all_gather.58 = bf16[64,4096]{1,0:T(8,128)(2,1)S(1)} all-gather(bf16[64,1024]{1,0:T(8,128)(2,1)S(1)} %fusion.63), channel_id=1, replica_groups=mesh['section'=2,'blk'=16,'mp'=4] {'mp'}, dimensions={1}, use_global_device_ids=true | all-gather | bytes 655360 | tf_op jit(solution)/shard_map/all_gather | solution.py:110
  207.2 4.7 copy.37
  213.1 21.3 %all_gather.61 = bf16[1024,1,128]{2,0,1:T(8,128)(2,1)S(1)} all-gather(bf16[64,1,128]{2,0,1:T(8,128)(2,1)S(1)} %pad_maximum_fusion), channel_id=1, replica_groups=mesh['section'=2,'blk'=16,'mp'=4] {'blk'}, dimensions={0}, use_global_device_ids=true | all-gather | bytes 278528 | tf_op jit(solution)/shard_map/all_gather | solution.py:132
  234.3 24.3 %all-gather = bf16[1024,1,1,128]{3,0,2,1:T(8,128)(2,1)S(1)} all-gather(bf16[64,1,1,128]{3,0,2,1:T(8,128)(2,1)S(1)} %slice.285), channel_id=2, replica_groups=mesh['section'=2,'blk'=16,'mp'=4] {'blk'}, dimensions={0}, use_global_device_ids=true | all-gather | bytes 278528 | tf_op jit(solution)/shard_map/all_gather | solution.py:133
  262.4 11.4 %copy.31 = bf16[1024,4096]{1,0:T(8,128)(2,1)} copy(bf16[1024,4096]{0,1:T(8,128)(2,1)} %bitcast.333) | data formatting | bytes 16777216 | tf_op jit(solution)/shard_map/dot_general | solution.py:118
  273.8 6.1 fusion.125
  283.8 5.8 fusion.13
  292.8 15.5 %reduce-scatter.6.cloned.1.call-done = bf16[64,1024]{1,0:T(8,128)(2,1)} async-done(((bf16[64,4096]{1,0:T(8,128)(2,1)}), bf16[64,1024]{1,0:T(8,128)(2,1)}) %reduce-scatter.6.cloned.1.call-update) | async-done | bytes 131088 | tf_op jit(solution)/shard_map/reduce_scatter | solution.py:165
  313.6 13.5 %all_gather.64 = bf16[64,4096]{1,0:T(8,128)(2,1)S(1)} all-gather(bf16[64,1024]{1,0:T(8,128)(2,1)S(1)} %fusion.65), channel_id=1, replica_groups=mesh['section'=2,'blk'=16,'mp'=4] {'mp'}, dimensions={1}, use_global_device_ids=true | all-gather | bytes 655360 | tf_op jit(solution)/shard_map/all_gather | solution.py:110
  328.2 6.1 fusion.128
  334.3 23.7 %all-gather.1 = bf16[1024,1,1,128]{3,0,2,1:T(8,128)(2,1)S(1)} all-gather(bf16[64,1,1,128]{3,0,2,1:T(8,128)(2,1)S(1)} %slice.284), channel_id=3, replica_groups=mesh['section'=2,'blk'=16,'mp'=4] {'blk'}, dimensions={0}, use_global_device_ids=true | all-gather | bytes 278528 | tf_op jit(solution)/shard_map/all_gather | solution.py:133
  358.3 23.3 %all_gather.66 = bf16[1024,1,128]{2,0,1:T(8,128)(2,1)S(1)} all-gather(bf16[64,1,128]{2,0,1:T(8,128)(2,1)S(1)} %pad_maximum_fusion.1), channel_id=1, replica_groups=mesh['section'=2,'blk'=16,'mp'=4] {'blk'}, dimensions={0}, use_global_device_ids=true | all-gather | bytes 278528 | tf_op jit(solution)/shard_map/all_gather | solution.py:132
  397.1 15.1 %reduce-scatter.8.cloned.1.call-done = bf16[64,1024]{1,0:T(8,128)(2,1)} async-done(((bf16[64,4096]{1,0:T(8,128)(2,1)}), bf16[64,1024]{1,0:T(8,128)(2,1)}) %reduce-scatter.8.cloned.1.call-update) | async-done | bytes 131088 | tf_op jit(solution)/shard_map/reduce_scatter | solution.py:165
  415.7 13.4 %all_gather.67 = bf16[64,4096]{1,0:T(8,128)(2,1)S(1)} all-gather(bf16[64,1024]{1,0:T(8,128)(2,1)S(1)} %broadcast_select_fusion.2), channel_id=1, replica_groups=mesh['section'=2,'blk'=16,'mp'=4] {'mp'}, dimensions={1}, use_global_device_ids=true | all-gather | bytes 655360 | tf_op jit(solution)/shard_map/all_gather | solution.py:110
  430.2 6.1 fusion.131
  436.3 23.7 %all-gather.2 = bf16[1024,1,1,128]{3,0,2,1:T(8,128)(2,1)S(1)} all-gather(bf16[64,1,1,128]{3,0,2,1:T(8,128)(2,1)S(1)} %slice.283), channel_id=4, replica_groups=mesh['section'=2,'blk'=16,'mp'=4] {'blk'}, dimensions={0}, use_global_device_ids=true | all-gather | bytes 278528 | tf_op jit(solution)/shard_map/all_gather | solution.py:133
  460.3 23.4 %all_gather.69 = bf16[1024,1,128]{2,0,1:T(8,128)(2,1)S(1)} all-gather(bf16[64,1,128]{2,0,1:T(8,128)(2,1)S(1)} %pad_maximum_fusion.2), channel_id=1, replica_groups=mesh['section'=2,'blk'=16,'mp'=4] {'blk'}, dimensions={0}, use_global_device_ids=true | all-gather | bytes 278528 | tf_op jit(solution)/shard_map/all_gather | solution.py:132
  497.4 17.7 %reduce-scatter.10.cloned.1.call-done = bf16[64,1024]{1,0:T(8,128)(2,1)} async-done(((bf16[64,4096]{1,0:T(8,128)(2,1)}), bf16[64,1024]{1,0:T(8,128)(2,1)}) %reduce-scatter.10.cloned.1.call-update) | async-done | bytes 131088 | tf_op jit(solution)/shard_map/reduce_scatter | solution.py:165
  519.3 13.4 %all_gather.70 = bf16[64,4096]{1,0:T(8,128)(2,1)S(1)} all-gather(bf16[64,1024]{1,0:T(8,128)(2,1)S(1)} %broadcast_select_fusion.1), channel_id=1, replica_groups=mesh['section'=2,'blk'=16,'mp'=4] {'mp'}, dimensions={1}, use_global_device_ids=true | all-gather | bytes 655360 | tf_op jit(solution)/shard_map/all_gather | solution.py:110
  533.7 6.1 fusion.134
  539.8 23.8 %all-gather.3 = bf16[1024,1,1,128]{3,0,2,1:T(8,128)(2,1)S(1)} all-gather(bf16[64,1,1,128]{3,0,2,1:T(8,128)(2,1)S(1)} %slice.282), channel_id=5, replica_groups=mesh['section'=2,'blk'=16,'mp'=4] {'blk'}, dimensions={0}, use_global_device_ids=true | all-gather | bytes 278528 | tf_op jit(solution)/shard_map/all_gather | solution.py:133
  563.9 23.2 %all_gather.72 = bf16[1024,1,128]{2,0,1:T(8,128)(2,1)S(1)} all-gather(bf16[64,1,128]{2,0,1:T(8,128)(2,1)S(1)} %pad_maximum_fusion.3), channel_id=1, replica_groups=mesh['section'=2,'blk'=16,'mp'=4] {'blk'}, dimensions={0}, use_global_device_ids=true | all-gather | bytes 278528 | tf_op jit(solution)/shard_map/all_gather | solution.py:132
  600.3 18.8 %reduce-scatter.12.cloned.1.call-done = bf16[64,1024]{1,0:T(8,128)(2,1)} async-done(((bf16[64,4096]{1,0:T(8,128)(2,1)}), bf16[64,1024]{1,0:T(8,128)(2,1)}) %reduce-scatter.12.cloned.1.call-update) | async-done | bytes 131088 | tf_op jit(solution)/shard_map/reduce_scatter | solution.py:165
  625.7 12.8 %all_gather.73 = bf16[64,4096]{1,0:T(8,128)(2,1)S(1)} all-gather(bf16[64,1024]{1,0:T(8,128)(2,1)S(1)} %broadcast_select_fusion), channel_id=1, replica_groups=mesh['section'=2,'blk'=16,'mp'=4] {'mp'}, dimensions={1}, use_global_device_ids=true | all-gather | bytes 655360 | tf_op jit(solution)/shard_map/all_gather | solution.py:110
  639.5 6.1 fusion.137
  645.6 23.7 %all-gather.4 = bf16[1024,1,1,128]{3,0,2,1:T(8,128)(2,1)S(1)} all-gather(bf16[64,1,1,128]{3,0,2,1:T(8,128)(2,1)S(1)} %slice.281), channel_id=6, replica_groups=mesh['section'=2,'blk'=16,'mp'=4] {'blk'}, dimensions={0}, use_global_device_ids=true | all-gather | bytes 278528 | tf_op jit(solution)/shard_map/all_gather | solution.py:133
  669.6 23.3 %all_gather.75 = bf16[1024,1,128]{2,0,1:T(8,128)(2,1)S(1)} all-gather(bf16[64,1,128]{2,0,1:T(8,128)(2,1)S(1)} %pad_maximum_fusion.4), channel_id=1, replica_groups=mesh['section'=2,'blk'=16,'mp'=4] {'blk'}, dimensions={0}, use_global_device_ids=true | all-gather | bytes 278528 | tf_op jit(solution)/shard_map/all_gather | solution.py:132
  703.7 18.1 %reduce-scatter.14.cloned.1.call-done = bf16[64,1024]{1,0:T(8,128)(2,1)} async-done(((bf16[64,4096]{1,0:T(8,128)(2,1)}), bf16[64,1024]{1,0:T(8,128)(2,1)}) %reduce-scatter.14.cloned.1.call-update) | async-done | bytes 131088 | tf_op jit(solution)/shard_map/reduce_scatter | solution.py:165
  (313 shorter events, 105.0 us)
Async XLA Ops:
  7.4 74.5 %all-reduce.3.cloned.1.call-start = ((), (), s32[]{:S(2)}) async-start(), calls=%async_computation.5 | async-start | bytes 4194304 | tf_op jit(solution)/shard_map/psum | solution.py:11
  20.2 172.7 %copy-start.26 = (s32[256]{0:T(256)S(1)}, s32[256]{0:T(256)}, u32[]{:S(2)}) copy-start(s32[256]{0:T(256)} %param.18) | copy-start | bytes 3076
  20.3 186.9 %all-gather.9.cloned.1.call-start = ((), (), s32[]{:S(2)}) async-start(), calls=%async_computation.6 | async-start | bytes 2228224 | tf_op jit(solution)/shard_map/all_gather | solution.py:79
  20.9 241.5 %all-gather.11.cloned.1.call-start = ((), (), s32[]{:S(2)}) async-start(), calls=%async_computation.7 | async-start | bytes 8912896 | tf_op jit(solution)/shard_map/all_gather | solution.py:78
  21.4 262.3 %all-gather.13.cloned.1.call-start = ((), (), s32[]{:S(2)}) async-start(), calls=%async_computation.8 | async-start | bytes 8912896 | tf_op jit(solution)/shard_map/all_gather | solution.py:80
  22.0 286.3 %reduce-scatter.6.cloned.1.call-start = ((), (), s32[]{:S(2)}) async-start(), calls=%async_computation.9 | async-start | bytes 655360 | tf_op jit(solution)/shard_map/reduce_scatter | solution.py:165
  22.1 168.5 %copy-start.47 = (f32[64]{0:T(128)}, f32[64]{0:T(128)S(1)}, u32[]{:S(2)}) copy-start(f32[64]{0:T(128)S(1)} %get-tuple-element.74) | copy-start | bytes 772
  22.9 335.1 %copy-start.27 = (f32[64]{0:T(128)}, f32[64]{0:T(128)S(1)}, u32[]{:S(2)}) copy-start(f32[64]{0:T(128)S(1)} %multiply_exponential_fusion) | copy-start | bytes 772
  23.0 167.7 %copy-start.45 = (s32[64]{0:T(128)}, s32[64]{0:T(128)S(1)}, u32[]{:S(2)}) copy-start(s32[64]{0:T(128)S(1)} %iota_add_fusion.5) | copy-start | bytes 772
  23.0 189.0 %copy-start.30 = (s32[64]{0:T(128)}, s32[64]{0:T(128)S(1)}, u32[]{:S(2)}) copy-start(s32[64]{0:T(128)S(1)} %get-tuple-element.77) | copy-start | bytes 772
  23.0 167.7 %copy-start.41 = (f32[64]{0:T(128)}, f32[64]{0:T(128)S(1)}, u32[]{:S(2)}) copy-start(f32[64]{0:T(128)S(1)} %get-tuple-element.80) | copy-start | bytes 772
  23.0 167.7 %copy-start.43 = (f32[64]{0:T(128)}, f32[64]{0:T(128)S(1)}, u32[]{:S(2)}) copy-start(f32[64]{0:T(128)S(1)} %get-tuple-element.79) | copy-start | bytes 772
  23.0 167.7 %copy-start.33 = (s32[64]{0:T(128)}, s32[64]{0:T(128)S(1)}, u32[]{:S(2)}) copy-start(s32[64]{0:T(128)S(1)} %get-tuple-element.75) | copy-start | bytes 772
  23.0 167.7 %copy-start.35 = (s32[64]{0:T(128)}, s32[64]{0:T(128)S(1)}, u32[]{:S(2)}) copy-start(s32[64]{0:T(128)S(1)} %get-tuple-element.76) | copy-start | bytes 772
  23.1 167.7 %copy-start.37 = (f32[64]{0:T(128)}, f32[64]{0:T(128)S(1)}, u32[]{:S(2)}) copy-start(f32[64]{0:T(128)S(1)} %get-tuple-element.82) | copy-start | bytes 772
  23.1 167.7 %copy-start.39 = (f32[64]{0:T(128)}, f32[64]{0:T(128)S(1)}, u32[]{:S(2)}) copy-start(f32[64]{0:T(128)S(1)} %get-tuple-element.81) | copy-start | bytes 772
  289.6 122.6 %reduce-scatter.8.cloned.1.call-start = ((), (), s32[]{:S(2)}) async-start(), calls=%async_computation.10 | async-start | bytes 655360 | tf_op jit(solution)/shard_map/reduce_scatter | solution.py:165
  309.3 2.4 collective-permute-start
  328.1 56.9 %copy-start.21 = (f32[64,64]{1,0:T(8,128)S(1)}, f32[64,64]{1,0:T(8,128)}, u32[]{:S(2)}) copy-start(f32[64,64]{1,0:T(8,128)} %get-tuple-element.51) | copy-start | bytes 49156
  328.1 56.9 %copy-start.22 = (f32[64,64]{1,0:T(8,128)S(1)}, f32[64,64]{1,0:T(8,128)}, u32[]{:S(2)}) copy-start(f32[64,64]{1,0:T(8,128)} %get-tuple-element.52) | copy-start | bytes 49156
  328.1 57.0 %copy-start.14 = (pred[64,2048]{1,0:T(8,128)(4,1)S(1)}, pred[64,2048]{1,0:T(8,128)(4,1)}, u32[]{:S(2)}) copy-start(pred[64,2048]{1,0:T(8,128)(4,1)} %compare_and_fusion.1) | copy-start | bytes 393220
  393.4 121.7 %reduce-scatter.10.cloned.1.call-start = ((), (), s32[]{:S(2)}) async-start(), calls=%async_computation.11 | async-start | bytes 655360 | tf_op jit(solution)/shard_map/reduce_scatter | solution.py:165
  413.2 2.5 collective-permute-start.1
  430.2 57.0 %copy-start.19 = (f32[64,64]{1,0:T(8,128)S(1)}, f32[64,64]{1,0:T(8,128)}, u32[]{:S(2)}) copy-start(f32[64,64]{1,0:T(8,128)} %get-tuple-element.53) | copy-start | bytes 49156
  430.2 57.0 %copy-start.20 = (f32[64,64]{1,0:T(8,128)S(1)}, f32[64,64]{1,0:T(8,128)}, u32[]{:S(2)}) copy-start(f32[64,64]{1,0:T(8,128)} %get-tuple-element.54) | copy-start | bytes 49156
  430.2 57.2 %copy-start.13 = (pred[64,3072]{1,0:T(8,128)(4,1)S(1)}, pred[64,3072]{1,0:T(8,128)(4,1)}, u32[]{:S(2)}) copy-start(pred[64,3072]{1,0:T(8,128)(4,1)} %compare_and_fusion) | copy-start | bytes 589828
  496.2 122.9 %reduce-scatter.12.cloned.1.call-start = ((), (), s32[]{:S(2)}) async-start(), calls=%async_computation.12 | async-start | bytes 655360 | tf_op jit(solution)/shard_map/reduce_scatter | solution.py:165
  516.1 2.5 collective-permute-start.2
  533.7 56.9 %copy-start.17 = (f32[64,64]{1,0:T(8,128)S(1)}, f32[64,64]{1,0:T(8,128)}, u32[]{:S(2)}) copy-start(f32[64,64]{1,0:T(8,128)} %get-tuple-element.55) | copy-start | bytes 49156
  533.7 57.0 %copy-start.3 = (pred[64,4096]{1,0:T(8,128)(4,1)S(1)}, pred[64,4096]{1,0:T(8,128)(4,1)}, u32[]{:S(2)}) copy-start(pred[64,4096]{1,0:T(8,128)(4,1)} %get-tuple-element.40) | copy-start | bytes 786436
  600.2 121.5 %reduce-scatter.14.cloned.1.call-start = ((), (), s32[]{:S(2)}) async-start(), calls=%async_computation.13 | async-start | bytes 655360 | tf_op jit(solution)/shard_map/reduce_scatter | solution.py:165
  620.1 4.9 collective-permute-start.3
  (52 other events, 733.6 us)
Sparse Core Ops, SparseCore 0:
  20.4 61.4 all-reduce.2
  289.7 18.5 reduce-scatter.5
  393.5 18.7 reduce-scatter.7
  496.3 18.7 reduce-scatter.9
  600.3 18.6 reduce-scatter.11
  703.0 18.6 reduce-scatter.13
Sparse Core Ops, SparseCore 1:
  23.1 47.4 all-gather.8
  72.8 99.5 all-gather.10
  174.6 79.8 all-gather.12
